TPU v7x, 32 devices: a whole 2x2x4 slice. The times are simulated.
32 devices in a mesh: group: 2 (over y), samp: 4 (over z), band: 4 (over x, core).
Axes of the slice: x: 2, y: 2, z: 4, core: 2. Of those that a mesh axis runs over, the one named last changes fastest.
Arguments:
- features: bfloat16 [48, 8, 32, 256], P(None, ('group', 'samp'), 'band'), parts along dimension 1, may hold values from -6 to 6
- radiance: float32 [3, 8, 32, 256], P(None, ('group', 'samp'), 'band'), parts along dimension 1, may hold values from 0.02 to 16
- sample_order: int32 [8, 32, 32, 8], P(('group', 'samp'), 'band'), parts along dimension 0, may hold values from 0 to 7, each once within a row
- embed_first: bfloat16 [128, 48], replicated, may hold values from -0.875 to 0.875
- embed_second: bfloat16 [128, 128], replicated, may hold values from -0.5 to 0.5
- embed_third: bfloat16 [32, 128], replicated, may hold values from -0.5 to 0.5
- conv_first: bfloat16 [128, 800], replicated, may hold values from -0.21875 to 0.21875
- conv_second: bfloat16 [32, 128], replicated, may hold values from -0.5 to 0.5
- kernel_first: bfloat16 [128, 64], replicated, may hold values from -0.75 to 0.75
- kernel_second: bfloat16 [25, 128], replicated, may hold values from -0.5 to 0.5
Outputs:
- denoised: float32 [3, 64, 256], P(None, ('group', 'band'), 'samp'), parts along dimension 1
There are 2 independent parts, one for each index of `group`. A program takes and returns all parts, laid end to end along the dimension named above; an argument that names none is the same for every part. Nothing has to cross between parts.
Inputs may be any that keep to these rules, and one draw needn't show every extreme that they name: `sample_order`: the 8 entries of each tile (the last dimension) are a permutation of 0 to 7; along a crop row each value appears once in every tile.
All inputs are finite; a program needn't handle non-finite values.
Results may differ from a plain program's by a relative error of at most 0.0003.
The roundings to bfloat16 on the way count: a program that leaves them out, or rounds other values in their place, can miss the bound.
Values may be sent and summed in bfloat16 or wider, within the bound.
A program may use at most 64 MiB of HBM per device.

v0:
```python
import functools
import math

import jax
import jax.numpy as jnp
from jax import lax
from jax.experimental import pallas as pl
from jax.experimental.pallas import tpu as pltpu
from jax.sharding import PartitionSpec as P

KSIZE = 5
LANES = 128
SENT = jnp.bfloat16


def padded_2(cells, sides, width):
    for axis, dim in sides:
        count = lax.axis_size(axis)
        ends = count - 1
        head = lax.slice_in_dim(cells, 0, width, axis=dim)
        tail = lax.slice_in_dim(cells, cells.shape[dim] - width, cells.shape[dim], axis=dim)
        cells = jnp.concatenate(
            [
                lax.ppermute(tail, axis, [(i, (i + 1) % count) for i in range(ends)]),
                cells,
                lax.ppermute(head, axis, [((i + 1) % count, i) for i in range(ends)]),
            ],
            axis=dim,
        )
    return cells


def passed_along(block, axis, distance):
    devices = range(lax.axis_size(axis))
    route = [(i - distance, i) for i in devices if i - distance in devices]
    return lax.ppermute(block, axis, route)


def to_pixels(values, sample_order):
    tile_size = sample_order.shape[-1]
    dest_cols = sample_order.reshape(sample_order.shape[:-2] + (-1,))
    offsets = jnp.arange(dest_cols.shape[-1], dtype=jnp.int32) % tile_size
    result = jnp.zeros_like(values)
    for slot_id in range(tile_size):
        spread = jnp.repeat(values[..., slot_id::tile_size], tile_size, axis=-1)
        target = jnp.repeat(dest_cols[..., slot_id::tile_size], tile_size, axis=-1)
        result = jnp.where((target == offsets)[None], spread, result)
    return result


def embed_samples(columns, embed_first, embed_second, embed_third):
    layer_one = jax.nn.relu(
        jnp.dot(embed_first, columns, preferred_element_type=jnp.float32)
    ).astype(jnp.bfloat16)
    layer_two = jax.nn.relu(
        jnp.dot(embed_second, layer_one, preferred_element_type=jnp.float32)
    ).astype(jnp.bfloat16)
    return jnp.dot(embed_third, layer_two, preferred_element_type=jnp.float32)


def convolve(padded, row_count, col_count, conv_first, conv_second):
    shifted = [
        padded[:, row_off : row_off + row_count, col_off : col_off + col_count]
        for row_off in range(KSIZE)
        for col_off in range(KSIZE)
    ]
    stacked = jnp.stack(shifted).reshape(-1, row_count * col_count)
    hidden = jax.nn.relu(jnp.dot(conv_first, stacked, preferred_element_type=jnp.float32)).astype(
        jnp.bfloat16
    )
    result = jnp.dot(conv_second, hidden, preferred_element_type=jnp.float32).astype(jnp.bfloat16)
    return result.reshape(-1, row_count, col_count)


def shards(
    features,
    radiance,
    sample_order,
    embed_first,
    embed_second,
    embed_third,
    conv_first,
    conv_second,
    kernel_first,
    kernel_second,
):
    ordered = to_pixels(features, sample_order)
    lights = to_pixels(radiance, sample_order)
    channels, samples_dev, row_count, crop_width = ordered.shape
    emb_width = embed_third.shape[0]
    radius = KSIZE // 2
    scaling = 1.0 / math.sqrt(samples_dev * lax.axis_size("samp"))
    embedded = embed_samples(ordered.reshape(channels, -1), embed_first, embed_second, embed_third)
    emb_bf = embedded.astype(jnp.bfloat16)
    own_part = jnp.dot(kernel_first[:, :emb_width], emb_bf, preferred_element_type=jnp.float32)
    own_part = own_part.reshape(-1, samples_dev, row_count, crop_width)
    partial_value = jnp.sum(embedded.reshape(emb_width, samples_dev, row_count, crop_width), axis=1)
    summed_emb = lax.psum(partial_value, "samp")
    pooled = (summed_emb * scaling).astype(jnp.bfloat16)
    padded = padded_2(pooled, (("band", 1),), 2)
    padded = jnp.pad(padded, ((0, 0), (0, 0), (radius, radius)))
    context = convolve(padded, row_count, crop_width, conv_first, conv_second)
    col_count = context.shape[2]
    ctx_part = jnp.dot(
        kernel_first[:, emb_width:],
        context.reshape(emb_width, -1),
        preferred_element_type=jnp.float32,
    )
    ctx_part = ctx_part.reshape(-1, 1, row_count, col_count)
    hidden = jax.nn.relu(own_part + ctx_part).astype(jnp.bfloat16)
    logits = jnp.dot(
        kernel_second, hidden.reshape(hidden.shape[0], -1), preferred_element_type=jnp.float32
    )
    weights = jnp.exp(logits).reshape(-1, samples_dev, row_count, col_count)
    with_ones = jnp.concatenate(
        [lights, jnp.ones((1, samples_dev, row_count, crop_width), jnp.float32)], axis=0
    )
    canvas = jnp.zeros((4, row_count + 2 * radius, crop_width + 2 * radius), jnp.float32)
    for row_off in range(KSIZE):
        for col_off in range(KSIZE):
            tap_index = row_off * KSIZE + col_off
            contrib = jnp.sum(weights[tap_index][None] * with_ones, axis=1)
            canvas = canvas.at[
                :, row_off : row_off + row_count, col_off : col_off + crop_width
            ].add(contrib)
    canvas = canvas[:, :, radius : radius + crop_width]
    summed_all = lax.psum_scatter(canvas, "samp", scatter_dimension=2, tiled=True)
    top_rims = summed_all[:, :radius]
    low_rims = summed_all[:, radius + row_count :]
    summed = summed_all[:, radius : radius + row_count]
    from_below = passed_along(top_rims, "band", -1)
    from_above = passed_along(low_rims, "band", 1)
    summed = summed.at[:, row_count - radius :].add(from_below)
    summed = summed.at[:, :radius].add(from_above)
    return summed[:3] / summed[3:4]


MESH = pl.DeviceIdType.MESH


def slots_to_sources(order, tile_size, width):
    rows, tiles, _ = order.shape
    flat = order.reshape(rows * tiles, tile_size).astype(jnp.float32).astype(jnp.bfloat16)
    slot = lax.broadcasted_iota(jnp.int32, (tile_size, width), 0)
    col = lax.broadcasted_iota(jnp.int32, (tile_size, width), 1)
    spread = jnp.where(slot == col % tile_size, 1.0, 0.0).astype(jnp.bfloat16)
    wide = jnp.dot(flat, spread, preferred_element_type=jnp.float32)
    tile_id = lax.broadcasted_iota(jnp.int32, (rows * tiles, width), 0) % tiles
    tile_of = lax.broadcasted_iota(jnp.int32, (rows * tiles, width), 1) // tile_size
    wide = jnp.where(tile_id == tile_of, wide, 0.0)
    dest = jnp.sum(wide.reshape(rows, tiles, width), axis=1).astype(jnp.int32)
    col = lax.broadcasted_iota(jnp.int32, (rows, width), 1)
    offset = col % tile_size
    source = col
    for step in range(1 - tile_size, tile_size):
        near = dest if step == 0 else pltpu.roll(dest, (-step) % width, 1)
        inside = (offset + step >= 0) & (offset + step < tile_size)
        source = jnp.where((near == offset) & inside, col + step, source)
    return source


def fused(
    count,
    bands,
    scaling,
    feat_ref,
    rad_ref,
    order_ref,
    first_ref,
    second_ref,
    third_ref,
    conv_one_ref,
    conv_two_ref,
    kern_one_ref,
    kern_two_ref,
    out_ref,
    plane,
    light,
    emb,
    emb_bf,
    part,
    part_in,
    pooled,
    taps,
    logit,
    canvas,
    block,
    block_in,
    rim,
    rim_in,
    rs_send,
    rs_recv,
    ag_send,
    ag_recv,
    halo_send,
    halo_recv,
    cs_send,
    cs_recv,
    rim_send,
    rim_recv,
):
    channels, _, rows, width = feat_ref.shape
    tile_size = order_ref.shape[-1]
    emb_width = third_ref.shape[0]
    radius = KSIZE // 2
    share = rows // count
    tall = rows + 2 * radius
    cols = width // count
    lanes = block.shape[-1]
    fold = lanes // cols
    groups = 4 // fold
    me = lax.axis_index("samp")
    here = lax.axis_index("band")
    peers = [lax.rem(me + step, count) for step in range(1, count)]
    has_above = here > 0
    has_below = here < bands - 1

    barrier = pltpu.get_barrier_semaphore()
    for peer in peers:
        pl.semaphore_signal(barrier, inc=1, device_id={"samp": peer}, device_id_type=MESH)

    @pl.when(has_above)
    def _():
        pl.semaphore_signal(barrier, inc=1, device_id={"band": here - 1}, device_id_type=MESH)

    @pl.when(has_below)
    def _():
        pl.semaphore_signal(barrier, inc=1, device_id={"band": here + 1}, device_id_type=MESH)

    source = slots_to_sources(order_ref[0], tile_size, width)
    halves = []
    for start in range(0, width, lanes):
        halves.append((start, source[:, start : start + lanes] - start))

    def reorder(values):
        return [
            jnp.take_along_axis(
                values[:, start : start + lanes], index, axis=1, mode="promise_in_bounds"
            )
            for start, index in halves
        ]

    def strided(ref, start, size, stride):
        return jnp.concatenate(
            [ref[half, pl.ds(start, size, stride=stride), :] for half in range(ref.shape[0])],
            axis=1,
        )

    for chan in range(channels):
        for half, part_x in enumerate(reorder(feat_ref[chan, 0].astype(jnp.float32))):
            plane[half, chan * rows : (chan + 1) * rows, :] = part_x
    for chan in range(3):
        light[chan] = jnp.concatenate(reorder(rad_ref[chan, 0]), axis=1)

    for row in range(rows):
        x = strided(plane, row, channels, rows).astype(jnp.bfloat16)
        x = jnp.dot(first_ref[...], x, preferred_element_type=jnp.float32)
        x = jnp.maximum(x, 0.0).astype(jnp.bfloat16)
        x = jnp.dot(second_ref[...], x, preferred_element_type=jnp.float32)
        x = jnp.maximum(x, 0.0).astype(jnp.bfloat16)
        x = jnp.dot(third_ref[...], x, preferred_element_type=jnp.float32)
        emb[row] = x
        emb_bf[row] = x.astype(jnp.bfloat16)
        part[row] = x.astype(part.dtype)

    beside = jnp.minimum(here, 1) + jnp.minimum(bands - 1 - here, 1)
    pl.semaphore_wait(barrier, count - 1 + beside)

    sums = []
    for slot, peer in enumerate(peers):
        copy = pltpu.make_async_remote_copy(
            src_ref=part.at[pl.ds(peer * share, share)],
            dst_ref=part_in.at[slot],
            send_sem=rs_send.at[slot],
            recv_sem=rs_recv.at[slot],
            device_id={"samp": peer},
            device_id_type=MESH,
        )
        copy.start()
        sums.append(copy)
    total = emb[pl.ds(me * share, share)]
    for slot, copy in enumerate(sums):
        copy.wait_recv()
        total = total + part_in[slot].astype(jnp.float32)
    own = pl.ds(radius + me * share, share)
    pooled[own] = (total * scaling).astype(jnp.bfloat16)
    gathers = []
    for slot, peer in enumerate(peers):
        copy = pltpu.make_async_remote_copy(
            src_ref=pooled.at[own],
            dst_ref=pooled.at[own],
            send_sem=ag_send.at[slot],
            recv_sem=ag_recv.at[slot],
            device_id={"samp": peer},
            device_id_type=MESH,
        )
        copy.start()
        gathers.append(copy)
    for chan in range(4):
        canvas[chan] = jnp.zeros(canvas.shape[1:], jnp.float32)
    for copy in sums:
        copy.wait_send()
    for copy in gathers:
        copy.wait_recv()

    def halo(down):
        start = rows if down else radius
        goal = 0 if down else rows + radius
        return pltpu.make_async_remote_copy(
            src_ref=pooled.at[pl.ds(start, radius)],
            dst_ref=pooled.at[pl.ds(goal, radius)],
            send_sem=halo_send.at[int(down)],
            recv_sem=halo_recv.at[int(down)],
            device_id={"band": here + 1 if down else here - 1},
            device_id_type=MESH,
        )

    @pl.when(has_below)
    def _():
        halo(True).start()

    @pl.when(has_above)
    def _():
        halo(False).start()

    @pl.when(here == 0)
    def _():
        pooled[0:radius] = jnp.zeros((radius, emb_width, width), jnp.bfloat16)

    @pl.when(here == bands - 1)
    def _():
        pooled[rows + radius : tall] = jnp.zeros((radius, emb_width, width), jnp.bfloat16)

    depth = KSIZE * emb_width
    col = lax.broadcasted_iota(jnp.int32, (emb_width, width), 1)

    def spread_row(row):
        values = pooled[row].astype(jnp.float32)
        for col_off in range(KSIZE):
            shift = col_off - radius
            if shift == 0:
                moved = values
            else:
                moved = pltpu.roll(values, (-shift) % width, 1)
                moved = jnp.where((col + shift >= 0) & (col + shift < width), moved, 0.0)
            start = row * depth + col_off * emb_width
            taps[start : start + emb_width, :] = moved.astype(jnp.bfloat16)

    def weigh_row(row):
        stacked = taps[row * depth : row * depth + KSIZE * depth, :]
        hidden = jnp.dot(conv_one_ref[...], stacked, preferred_element_type=jnp.float32)
        hidden = jnp.maximum(hidden, 0.0).astype(jnp.bfloat16)
        context = jnp.dot(conv_two_ref[...], hidden, preferred_element_type=jnp.float32)
        both = jnp.concatenate([emb_bf[row], context.astype(jnp.bfloat16)], axis=0)
        hidden = jnp.dot(kern_one_ref[...], both, preferred_element_type=jnp.float32)
        hidden = jnp.maximum(hidden, 0.0).astype(jnp.bfloat16)
        start = row * (logit.shape[1] // rows)
        values = jnp.dot(kern_two_ref[...], hidden, preferred_element_type=jnp.float32)
        for half in range(logit.shape[0]):
            logit[half, start : start + KSIZE * KSIZE, :] = values[
                :, half * lanes : (half + 1) * lanes
            ]

    for row in range(radius, rows + radius):
        spread_row(row)
    inner = range(radius, rows - radius)
    for row in inner:
        weigh_row(row)

    @pl.when(has_above)
    def _():
        halo(True).wait_recv()

    @pl.when(has_below)
    def _():
        halo(False).wait_recv()

    for row in range(tall):
        if row < radius or row >= rows + radius:
            spread_row(row)
    for row in range(rows):
        if row not in inner:
            weigh_row(row)

    col = lax.broadcasted_iota(jnp.int32, (rows, width), 1)
    colours = [light[chan] for chan in range(3)]
    stride = logit.shape[1] // rows
    for row_off in range(KSIZE):
        sums_c = [None] * 4
        for col_off in range(KSIZE):
            shift = col_off - radius
            weight = jnp.exp(strided(logit, row_off * KSIZE + col_off, rows, stride))
            if shift != 0:
                weight = jnp.where((col + shift >= 0) & (col + shift < width), weight, 0.0)
            for chan in range(4):
                term = weight * colours[chan] if chan < 3 else weight
                if shift != 0:
                    term = pltpu.roll(term, shift % width, 1)
                sums_c[chan] = term if sums_c[chan] is None else sums_c[chan] + term
        for chan in range(4):
            canvas[chan, row_off : row_off + rows, :] += sums_c[chan]

    lane = lax.broadcasted_iota(jnp.int32, (tall, lanes), 1) // cols
    for owner in range(count):
        base = owner * cols // lanes * lanes
        at = owner * cols - base
        for group in range(groups):
            packed = None
            for place in range(fold):
                piece = canvas[group * fold + place, 0:tall, base : base + lanes]
                turn = (place * cols - at) % lanes
                if turn:
                    piece = pltpu.roll(piece, turn, 1)
                packed = piece if packed is None else jnp.where(lane == place, piece, packed)
            block[owner, group * tall : (group + 1) * tall, :] = packed
    splats = []
    for slot, peer in enumerate(peers):
        copy = pltpu.make_async_remote_copy(
            src_ref=block.at[peer],
            dst_ref=block_in.at[slot],
            send_sem=cs_send.at[slot],
            recv_sem=cs_recv.at[slot],
            device_id={"samp": peer},
            device_id_type=MESH,
        )
        copy.start()
        splats.append(copy)
    for copy in gathers:
        copy.wait_send()

    @pl.when(has_below)
    def _():
        halo(True).wait_send()

    @pl.when(has_above)
    def _():
        halo(False).wait_send()

    total = block[me]
    for slot, copy in enumerate(splats):
        copy.wait_recv()
        total = total + block_in[slot]
    for copy in splats:
        copy.wait_send()

    for group in range(groups):
        rim[0, group * radius : (group + 1) * radius, :] = total[
            group * tall : group * tall + radius
        ]
        rim[1, group * radius : (group + 1) * radius, :] = total[
            group * tall + tall - radius : (group + 1) * tall
        ]

    def edge(down):
        return pltpu.make_async_remote_copy(
            src_ref=rim.at[int(down)],
            dst_ref=rim_in.at[int(down)],
            send_sem=rim_send.at[int(down)],
            recv_sem=rim_recv.at[int(down)],
            device_id={"band": here + 1 if down else here - 1},
            device_id_type=MESH,
        )

    @pl.when(has_below)
    def _():
        edge(True).start()

    @pl.when(has_above)
    def _():
        edge(False).start()

    @pl.when(here == 0)
    def _():
        rim_in[1] = jnp.zeros(rim_in.shape[1:], jnp.float32)

    @pl.when(here == bands - 1)
    def _():
        rim_in[0] = jnp.zeros(rim_in.shape[1:], jnp.float32)

    @pl.when(has_above)
    def _():
        edge(True).wait_recv()

    @pl.when(has_below)
    def _():
        edge(False).wait_recv()

    planes = []
    for group in range(groups):
        body = total[group * tall + radius : group * tall + radius + rows]
        above = rim_in[1, group * radius : (group + 1) * radius, :]
        below = rim_in[0, group * radius : (group + 1) * radius, :]
        gap = jnp.zeros((rows - 2 * radius, lanes), jnp.float32)
        body = body + jnp.concatenate([above, gap, below], axis=0)
        for place in range(fold):
            planes.append(pltpu.roll(body, lanes - place * cols, 1) if place else body)
    for chan in range(3):
        out_ref[chan] = (planes[chan] / planes[3])[:, :cols]

    @pl.when(has_below)
    def _():
        edge(True).wait_send()

    @pl.when(has_above)
    def _():
        edge(False).wait_send()


def fits(features, third, count):
    _, samples_dev, rows, width = features.shape
    radius = KSIZE // 2
    lanes = LANES
    cols = width // count
    return (
        samples_dev == 1
        and count > 1
        and rows % count == 0
        and rows % 8 == 0
        and rows >= 2 * radius
        and width % lanes == 0
        and lanes % cols == 0
        and lanes // cols in (1, 2, 4)
        and third.shape[0] % 16 == 0
    )


def fused_shards(
    features,
    radiance,
    sample_order,
    embed_first,
    embed_second,
    embed_third,
    conv_first,
    conv_second,
    kernel_first,
    kernel_second,
):
    count = lax.axis_size("samp")
    bands = lax.axis_size("band")
    channels, samples_dev, rows, width = features.shape
    emb_width = embed_third.shape[0]
    radius = KSIZE // 2
    tall = rows + 2 * radius
    cols = width // count
    groups = 4 * cols // LANES
    taps_pad = -(-KSIZE * KSIZE // 8) * 8
    scaling = 1.0 / math.sqrt(samples_dev * count)
    vmem = pl.BlockSpec(memory_space=pltpu.VMEM)
    sem = pltpu.SemaphoreType.DMA
    rim_rows = -(-groups * radius // 8) * 8
    return pl.pallas_call(
        functools.partial(fused, count, bands, scaling),
        out_shape=jax.ShapeDtypeStruct((3, rows, cols), jnp.float32),
        in_specs=[vmem] * 10,
        out_specs=vmem,
        scratch_shapes=[
            pltpu.VMEM((width // LANES, channels * rows, LANES), jnp.float32),
            pltpu.VMEM((3, rows, width), jnp.float32),
            pltpu.VMEM((rows, emb_width, width), jnp.float32),
            pltpu.VMEM((rows, emb_width, width), jnp.bfloat16),
            pltpu.VMEM((rows, emb_width, width), SENT),
            pltpu.VMEM((count - 1, rows // count, emb_width, width), SENT),
            pltpu.VMEM((tall, emb_width, width), jnp.bfloat16),
            pltpu.VMEM((tall * KSIZE * emb_width, width), jnp.bfloat16),
            pltpu.VMEM((width // LANES, rows * taps_pad, LANES), jnp.float32),
            pltpu.VMEM((4, -(-tall // 8) * 8, width), jnp.float32),
            pltpu.VMEM((count, groups * tall, LANES), jnp.float32),
            pltpu.VMEM((count - 1, groups * tall, LANES), jnp.float32),
            pltpu.VMEM((2, rim_rows, LANES), jnp.float32),
            pltpu.VMEM((2, rim_rows, LANES), jnp.float32),
            sem((count - 1,)),
            sem((count - 1,)),
            sem((count - 1,)),
            sem((count - 1,)),
            sem((2,)),
            sem((2,)),
            sem((count - 1,)),
            sem((count - 1,)),
            sem((2,)),
            sem((2,)),
        ],
        compiler_params=pltpu.CompilerParams(collective_id=0, has_side_effects=True),
    )(
        features,
        radiance,
        sample_order,
        embed_first,
        embed_second,
        embed_third,
        conv_first,
        conv_second,
        kernel_first,
        kernel_second,
    )


def either(*operands):
    if fits(operands[0], operands[5], lax.axis_size("samp")):
        return fused_shards(*operands)
    return shards(*operands)


def solution(mesh):
    in_specs = (
        P(None, ("group", "samp"), "band", None),
        P(None, ("group", "samp"), "band", None),
        P(("group", "samp"), "band", None, None),
        P(),
        P(),
        P(),
        P(),
        P(),
        P(),
        P(),
    )
    out_specs = P(None, ("group", "band"), "samp")
    return jax.shard_map(either, mesh=mesh, in_specs=in_specs, out_specs=out_specs, check_vma=False)
```

profile of v0, /device:TPU:1, one launch (start us, length us, event | category | flops | bytes accessed | tf_op | source)
XLA Modules:
  0.0 33.4 jit_solution(5231704634265500783)
XLA Ops:
  0.0 0.0 copy-start.1
  0.0 0.0 copy-start
  0.0 1.4 %copy.12.first_ref = bf16[128,48]{1,0:T(8,128)(2,1)} copy(bf16[128,48]{0,1:T(8,128)(2,1)} %param.13) | data formatting | bytes 24576 | tf_op args[3]
  1.5 0.0 copy-done.1
  1.5 0.7 %copy.14.kern_one_ref = bf16[128,64]{1,0:T(8,128)(2,1)} copy(bf16[128,64]{0,1:T(8,128)(2,1)S(1)} %copy-done.1) | data formatting | bytes 32768 | tf_op args[8]
  2.2 1.5 %copy.11.order_ref = s32[1,8,32,8]{3,2,1,0:T(8,128)} copy(s32[1,8,32,8]{2,3,1,0:T(8,128)} %param.12) | data formatting | bytes 16384 | tf_op args[2]
  3.7 0.0 copy-done
  3.7 0.8 %copy.13.conv_one_ref = bf16[128,800]{1,0:T(8,128)(2,1)} copy(bf16[128,800]{0,1:T(8,128)(2,1)S(1)} %copy-done) | data formatting | bytes 409600 | tf_op args[6]
  4.5 27.6 %shard_map.100 = f32[3,8,64]{2,1,0:T(8,128)} custom-call(bf16[48,1,8,256]{3,2,1,0:T(8,128)(2,1)} %feat_ref.1, f32[3,1,8,256]{3,2,1,0:T(8,128)} %rad_ref.1, s32[1,8,32,8]{3,2,1,0:T(8,128)} %copy.11.order_ref, bf16[128,48]{1,0:T(8,128)(2,1)} %copy.12.first_ref, bf16[128,128]{1,0:T(8,128)(2,1)} %second_ref.1, bf16[32,128]{1,0:T(8,128)(2,1)} %third_ref.1, ...), custom_call_target="tpu_custom_call" | custom-call | tf_op jit(solution)/shard_map/pallas_call | solution.py:552
  32.1 1.3 %copy.16 = f32[3,8,64]{2,1,0:T(8,128)} copy(f32[3,8,64]{2,1,0:T(8,128)} %shard_map.100) | data formatting | bytes 12288
Async XLA Ops:
  0.0 1.5 %copy-start.1 = (bf16[128,64]{0,1:T(8,128)(2,1)S(1)}, bf16[128,64]{0,1:T(8,128)(2,1)}, u32[]{:S(2)}) copy-start(bf16[128,64]{0,1:T(8,128)(2,1)} %param.18) | copy-start | bytes 49156
  0.0 3.7 %copy-start = (bf16[128,800]{0,1:T(8,128)(2,1)S(1)}, bf16[128,800]{0,1:T(8,128)(2,1)}, u32[]{:S(2)}) copy-start(bf16[128,800]{0,1:T(8,128)(2,1)} %param.16) | copy-start | bytes 614404
where the time goes:
time: 33.7 us; the launch traced here: 33.4 us
  Pallas kernels  27.6 us (82%)
  local copies, waits for them, and re-layouts  5.82 us (17%)
    pallas_call x1, Pallas kernels, fused_shards(): pl.pallas_call(functools.partial(fused, count, bands, scaling), out_shape...  27.6 us
    unnamed x9, local copies, waits for them, and re-layouts  5.82 us

commit v1 on v0

--- a/solution.py
+++ b/solution.py
@@ -10,7 +10,7 @@
 
 KSIZE = 5
 LANES = 128
-SENT = jnp.bfloat16
+SENT = jnp.float32
 
 
 def padded_2(cells, sides, width):
@@ -138,25 +138,25 @@
 MESH = pl.DeviceIdType.MESH
 
 
-def slots_to_sources(order, tile_size, width):
-    rows, tiles, _ = order.shape
-    flat = order.reshape(rows * tiles, tile_size).astype(jnp.float32).astype(jnp.bfloat16)
-    slot = lax.broadcasted_iota(jnp.int32, (tile_size, width), 0)
-    col = lax.broadcasted_iota(jnp.int32, (tile_size, width), 1)
-    spread = jnp.where(slot == col % tile_size, 1.0, 0.0).astype(jnp.bfloat16)
-    wide = jnp.dot(flat, spread, preferred_element_type=jnp.float32)
-    tile_id = lax.broadcasted_iota(jnp.int32, (rows * tiles, width), 0) % tiles
-    tile_of = lax.broadcasted_iota(jnp.int32, (rows * tiles, width), 1) // tile_size
-    wide = jnp.where(tile_id == tile_of, wide, 0.0)
-    dest = jnp.sum(wide.reshape(rows, tiles, width), axis=1).astype(jnp.int32)
+def slots_to_sources(order, width):
+    rows, tile_size, tiles = order.shape
+    flat = order.reshape(rows * tile_size, tiles).astype(jnp.float32).astype(jnp.bfloat16)
+    tile = lax.broadcasted_iota(jnp.int32, (tiles, width), 0)
+    col = lax.broadcasted_iota(jnp.int32, (tiles, width), 1)
+    spread = jnp.where(tile == col // tile_size, 1.0, 0.0).astype(jnp.bfloat16)
+    wide = jnp.dot(flat, spread, preferred_element_type=jnp.float32).astype(jnp.int32)
+    slot = lax.broadcasted_iota(jnp.int32, (rows * tile_size, width), 0) % tile_size
+    offset = lax.broadcasted_iota(jnp.int32, (rows * tile_size, width), 1) % tile_size
+    wide = jnp.where(wide == offset, slot, 0)
+    slots = jnp.sum(wide.reshape(rows, tile_size, width), axis=1)
     col = lax.broadcasted_iota(jnp.int32, (rows, width), 1)
-    offset = col % tile_size
-    source = col
-    for step in range(1 - tile_size, tile_size):
-        near = dest if step == 0 else pltpu.roll(dest, (-step) % width, 1)
-        inside = (offset + step >= 0) & (offset + step < tile_size)
-        source = jnp.where((near == offset) & inside, col + step, source)
-    return source
+    return col // tile_size * tile_size + slots
+
+
+def share_of(device, count):
+    if count % 2:
+        return device
+    return device + 1 - 2 * (device % 2)
 
 
 def fused(
@@ -166,17 +166,19 @@
     feat_ref,
     rad_ref,
     order_ref,
-    first_ref,
+    first_turned,
     second_ref,
     third_ref,
-    conv_one_ref,
+    conv_one_turned,
     conv_two_ref,
-    kern_one_ref,
+    kern_one_turned,
     kern_two_ref,
     out_ref,
+    first_ref,
+    conv_one_ref,
+    kern_one_ref,
     plane,
     light,
-    emb,
     emb_bf,
     part,
     part_in,
@@ -200,7 +202,6 @@
     rim_recv,
 ):
     channels, _, rows, width = feat_ref.shape
-    tile_size = order_ref.shape[-1]
     emb_width = third_ref.shape[0]
     radius = KSIZE // 2
     share = rows // count
@@ -212,6 +213,7 @@
     me = lax.axis_index("samp")
     here = lax.axis_index("band")
     peers = [lax.rem(me + step, count) for step in range(1, count)]
+    chunk = share_of(me, count)
     has_above = here > 0
     has_below = here < bands - 1
 
@@ -221,13 +223,25 @@
 
     @pl.when(has_above)
     def _():
-        pl.semaphore_signal(barrier, inc=1, device_id={"band": here - 1}, device_id_type=MESH)
+        for peer in [me] + peers:
+            pl.semaphore_signal(
+                barrier,
+                inc=1,
+                device_id={"samp": peer, "band": here - 1},
+                device_id_type=MESH,
+            )
 
     @pl.when(has_below)
     def _():
-        pl.semaphore_signal(barrier, inc=1, device_id={"band": here + 1}, device_id_type=MESH)
-
-    source = slots_to_sources(order_ref[0], tile_size, width)
+        for peer in [me] + peers:
+            pl.semaphore_signal(
+                barrier,
+                inc=1,
+                device_id={"samp": peer, "band": here + 1},
+                device_id_type=MESH,
+            )
+
+    source = slots_to_sources(order_ref[0], width)
     halves = []
     for start in range(0, width, lanes):
         halves.append((start, source[:, start : start + lanes] - start))
@@ -252,24 +266,28 @@
     for chan in range(3):
         light[chan] = jnp.concatenate(reorder(rad_ref[chan, 0]), axis=1)
 
-    for row in range(rows):
+    first_ref[...] = first_turned[...].T
+
+    def embed_row(row):
         x = strided(plane, row, channels, rows).astype(jnp.bfloat16)
         x = jnp.dot(first_ref[...], x, preferred_element_type=jnp.float32)
         x = jnp.maximum(x, 0.0).astype(jnp.bfloat16)
         x = jnp.dot(second_ref[...], x, preferred_element_type=jnp.float32)
         x = jnp.maximum(x, 0.0).astype(jnp.bfloat16)
         x = jnp.dot(third_ref[...], x, preferred_element_type=jnp.float32)
-        emb[row] = x
         emb_bf[row] = x.astype(jnp.bfloat16)
-        part[row] = x.astype(part.dtype)
+        return x
 
     beside = jnp.minimum(here, 1) + jnp.minimum(bands - 1 - here, 1)
-    pl.semaphore_wait(barrier, count - 1 + beside)
-
     sums = []
     for slot, peer in enumerate(peers):
+        start = share_of(peer, count) * share
+        for row in range(share):
+            part[slot, row] = embed_row(start + row).astype(part.dtype)
+        if slot == 0:
+            pl.semaphore_wait(barrier, count - 1 + beside * count)
         copy = pltpu.make_async_remote_copy(
-            src_ref=part.at[pl.ds(peer * share, share)],
+            src_ref=part.at[slot],
             dst_ref=part_in.at[slot],
             send_sem=rs_send.at[slot],
             recv_sem=rs_recv.at[slot],
@@ -278,30 +296,31 @@
         )
         copy.start()
         sums.append(copy)
-    total = emb[pl.ds(me * share, share)]
+    total = [embed_row(chunk * share + row) for row in range(share)]
+    conv_one_ref[...] = conv_one_turned[...].T
+    kern_one_ref[...] = kern_one_turned[...].T
+    canvas[...] = jnp.zeros(canvas.shape, jnp.float32)
     for slot, copy in enumerate(sums):
         copy.wait_recv()
-        total = total + part_in[slot].astype(jnp.float32)
-    own = pl.ds(radius + me * share, share)
-    pooled[own] = (total * scaling).astype(jnp.bfloat16)
-    gathers = []
-    for slot, peer in enumerate(peers):
-        copy = pltpu.make_async_remote_copy(
-            src_ref=pooled.at[own],
-            dst_ref=pooled.at[own],
+        for row in range(share):
+            total[row] = total[row] + part_in[slot, row].astype(jnp.float32)
+    for row in range(share):
+        pooled[radius + chunk * share + row] = (total[row] * scaling).astype(jnp.bfloat16)
+
+    def gather(slot, peer, sender):
+        rows_of = pl.ds(radius + share_of(sender, count) * share, share)
+        return pltpu.make_async_remote_copy(
+            src_ref=pooled.at[rows_of],
+            dst_ref=pooled.at[rows_of],
             send_sem=ag_send.at[slot],
-            recv_sem=ag_recv.at[slot],
+            recv_sem=ag_recv.at[sender],
             device_id={"samp": peer},
             device_id_type=MESH,
         )
+
+    gathers = [gather(slot, peer, me) for slot, peer in enumerate(peers)]
+    for copy in gathers:
         copy.start()
-        gathers.append(copy)
-    for chan in range(4):
-        canvas[chan] = jnp.zeros(canvas.shape[1:], jnp.float32)
-    for copy in sums:
-        copy.wait_send()
-    for copy in gathers:
-        copy.wait_recv()
 
     def halo(down):
         start = rows if down else radius
@@ -314,14 +333,6 @@
             device_id={"band": here + 1 if down else here - 1},
             device_id_type=MESH,
         )
-
-    @pl.when(has_below)
-    def _():
-        halo(True).start()
-
-    @pl.when(has_above)
-    def _():
-        halo(False).start()
 
     @pl.when(here == 0)
     def _():
@@ -361,8 +372,34 @@
                 :, half * lanes : (half + 1) * lanes
             ]
 
-    for row in range(radius, rows + radius):
-        spread_row(row)
+    edges = -(-radius // share)
+    order = list(range(edges)) + list(range(count - edges, count))
+    order = list(dict.fromkeys(order))
+    order += [share_id for share_id in range(count) if share_id not in order]
+    for place, share_id in enumerate(order):
+        owner = share_of(share_id, count)
+
+        @pl.when(me != owner)
+        def _():
+            gather(0, peers[0], owner).wait_recv()
+
+        if place == edges - 1:
+
+            @pl.when(has_above)
+            def _():
+                halo(False).start()
+
+        if place == min(2 * edges, count) - 1:
+
+            @pl.when(has_below)
+            def _():
+                halo(True).start()
+
+        if place >= min(2 * edges, count) - 1:
+            ready = order[: place + 1] if place == min(2 * edges, count) - 1 else [share_id]
+            for done in ready:
+                for row in range(share):
+                    spread_row(radius + done * share + row)
     inner = range(radius, rows - radius)
     for row in inner:
         weigh_row(row)
@@ -412,7 +449,31 @@
                 if turn:
                     piece = pltpu.roll(piece, turn, 1)
                 packed = piece if packed is None else jnp.where(lane == place, piece, packed)
-            block[owner, group * tall : (group + 1) * tall, :] = packed
+            block[owner, group * rows : (group + 1) * rows, :] = packed[radius : radius + rows]
+            at_rim = pl.ds(group * radius, radius)
+            rim[0, owner, at_rim, :] = packed[:radius]
+            rim[1, owner, at_rim, :] = packed[tall - radius :]
+
+    def edge(down, slot, peer):
+        return pltpu.make_async_remote_copy(
+            src_ref=rim.at[int(down), peer],
+            dst_ref=rim_in.at[int(down), slot],
+            send_sem=rim_send.at[int(down), slot],
+            recv_sem=rim_recv.at[int(down), slot],
+            device_id={"samp": peer, "band": here + 1 if down else here - 1},
+            device_id_type=MESH,
+        )
+
+    @pl.when(has_below)
+    def _():
+        for slot, peer in enumerate([me] + peers):
+            edge(True, slot, peer).start()
+
+    @pl.when(has_above)
+    def _():
+        for slot, peer in enumerate([me] + peers):
+            edge(False, slot, peer).start()
+
     splats = []
     for slot, peer in enumerate(peers):
         copy = pltpu.make_async_remote_copy(
@@ -425,7 +486,7 @@
         )
         copy.start()
         splats.append(copy)
-    for copy in gathers:
+    for copy in sums + gathers:
         copy.wait_send()
 
     @pl.when(has_below)
@@ -435,75 +496,58 @@
     @pl.when(has_above)
     def _():
         halo(False).wait_send()
+
+    @pl.when(here == 0)
+    def _():
+        rim_in[1] = jnp.zeros(rim_in.shape[1:], jnp.float32)
+
+    @pl.when(here == bands - 1)
+    def _():
+        rim_in[0] = jnp.zeros(rim_in.shape[1:], jnp.float32)
 
     total = block[me]
     for slot, copy in enumerate(splats):
         copy.wait_recv()
         total = total + block_in[slot]
-    for copy in splats:
-        copy.wait_send()
-
-    for group in range(groups):
-        rim[0, group * radius : (group + 1) * radius, :] = total[
-            group * tall : group * tall + radius
-        ]
-        rim[1, group * radius : (group + 1) * radius, :] = total[
-            group * tall + tall - radius : (group + 1) * tall
-        ]
-
-    def edge(down):
-        return pltpu.make_async_remote_copy(
-            src_ref=rim.at[int(down)],
-            dst_ref=rim_in.at[int(down)],
-            send_sem=rim_send.at[int(down)],
-            recv_sem=rim_recv.at[int(down)],
-            device_id={"band": here + 1 if down else here - 1},
-            device_id_type=MESH,
-        )
+
+    @pl.when(has_above)
+    def _():
+        for slot, peer in enumerate([me] + peers):
+            edge(True, slot, peer).wait_recv()
 
     @pl.when(has_below)
     def _():
-        edge(True).start()
-
-    @pl.when(has_above)
-    def _():
-        edge(False).start()
-
-    @pl.when(here == 0)
-    def _():
-        rim_in[1] = jnp.zeros(rim_in.shape[1:], jnp.float32)
-
-    @pl.when(here == bands - 1)
-    def _():
-        rim_in[0] = jnp.zeros(rim_in.shape[1:], jnp.float32)
-
-    @pl.when(has_above)
-    def _():
-        edge(True).wait_recv()
-
-    @pl.when(has_below)
-    def _():
-        edge(False).wait_recv()
+        for slot, peer in enumerate([me] + peers):
+            edge(False, slot, peer).wait_recv()
+
+    below = rim_in[0, 0]
+    above = rim_in[1, 0]
+    for slot in range(1, count):
+        below = below + rim_in[0, slot]
+        above = above + rim_in[1, slot]
 
     planes = []
     for group in range(groups):
-        body = total[group * tall + radius : group * tall + radius + rows]
-        above = rim_in[1, group * radius : (group + 1) * radius, :]
-        below = rim_in[0, group * radius : (group + 1) * radius, :]
+        near = slice(group * radius, (group + 1) * radius)
         gap = jnp.zeros((rows - 2 * radius, lanes), jnp.float32)
-        body = body + jnp.concatenate([above, gap, below], axis=0)
+        body = total[group * rows : (group + 1) * rows]
+        body = body + jnp.concatenate([above[near], gap, below[near]], axis=0)
         for place in range(fold):
             planes.append(pltpu.roll(body, lanes - place * cols, 1) if place else body)
     for chan in range(3):
         out_ref[chan] = (planes[chan] / planes[3])[:, :cols]
+    for copy in splats:
+        copy.wait_send()
 
     @pl.when(has_below)
     def _():
-        edge(True).wait_send()
+        for slot, peer in enumerate([me] + peers):
+            edge(True, slot, peer).wait_send()
 
     @pl.when(has_above)
     def _():
-        edge(False).wait_send()
+        for slot, peer in enumerate([me] + peers):
+            edge(False, slot, peer).wait_send()
 
 
 def fits(features, third, count):
@@ -555,42 +599,44 @@
         in_specs=[vmem] * 10,
         out_specs=vmem,
         scratch_shapes=[
+            pltpu.VMEM(embed_first.shape, jnp.bfloat16),
+            pltpu.VMEM(conv_first.shape, jnp.bfloat16),
+            pltpu.VMEM(kernel_first.shape, jnp.bfloat16),
             pltpu.VMEM((width // LANES, channels * rows, LANES), jnp.float32),
             pltpu.VMEM((3, rows, width), jnp.float32),
-            pltpu.VMEM((rows, emb_width, width), jnp.float32),
             pltpu.VMEM((rows, emb_width, width), jnp.bfloat16),
-            pltpu.VMEM((rows, emb_width, width), SENT),
+            pltpu.VMEM((count - 1, rows // count, emb_width, width), SENT),
             pltpu.VMEM((count - 1, rows // count, emb_width, width), SENT),
             pltpu.VMEM((tall, emb_width, width), jnp.bfloat16),
             pltpu.VMEM((tall * KSIZE * emb_width, width), jnp.bfloat16),
             pltpu.VMEM((width // LANES, rows * taps_pad, LANES), jnp.float32),
             pltpu.VMEM((4, -(-tall // 8) * 8, width), jnp.float32),
-            pltpu.VMEM((count, groups * tall, LANES), jnp.float32),
-            pltpu.VMEM((count - 1, groups * tall, LANES), jnp.float32),
-            pltpu.VMEM((2, rim_rows, LANES), jnp.float32),
-            pltpu.VMEM((2, rim_rows, LANES), jnp.float32),
+            pltpu.VMEM((count, groups * rows, LANES), jnp.float32),
+            pltpu.VMEM((count - 1, groups * rows, LANES), jnp.float32),
+            pltpu.VMEM((2, count, rim_rows, LANES), jnp.float32),
+            pltpu.VMEM((2, count, rim_rows, LANES), jnp.float32),
             sem((count - 1,)),
             sem((count - 1,)),
             sem((count - 1,)),
-            sem((count - 1,)),
+            sem((count,)),
             sem((2,)),
             sem((2,)),
             sem((count - 1,)),
             sem((count - 1,)),
-            sem((2,)),
-            sem((2,)),
+            sem((2, count)),
+            sem((2, count)),
         ],
         compiler_params=pltpu.CompilerParams(collective_id=0, has_side_effects=True),
     )(
         features,
         radiance,
-        sample_order,
-        embed_first,
+        jnp.swapaxes(sample_order, 2, 3),
+        embed_first.T,
         embed_second,
         embed_third,
-        conv_first,
+        conv_first.T,
         conv_second,
-        kernel_first,
+        kernel_first.T,
         kernel_second,
     )
 

time: 33.7 us -> 30.4 us (0.902)
  the two profiles are of different devices: /device:TPU:1 before, /device:TPU:0 now
where the time goes in v1:
time: 30.4 us; the launch traced here: 30.2 us
  Pallas kernels  28.8 us (95%)
  local copies, waits for them, and re-layouts  1.31 us (4%)
    pallas_call x1, Pallas kernels, fused_shards(): pl.pallas_call(functools.partial(fused, count, bands, scaling), out_shape...  28.8 us
    unnamed x1, local copies, waits for them, and re-layouts  1.31 us

profile of v1, /device:TPU:0, one launch (start us, length us, event | category | flops | bytes accessed | tf_op | source)
XLA Modules:
  0.0 30.2 jit_solution(10424335022032566018)
XLA Ops:
  0.0 28.8 %shard_map.100 = f32[3,8,64]{2,1,0:T(8,128)} custom-call(bf16[48,1,8,256]{3,2,1,0:T(8,128)(2,1)} %feat_ref.1, f32[3,1,8,256]{3,2,1,0:T(8,128)} %rad_ref.1, s32[1,8,8,32]{3,2,1,0:T(8,128)} %bitcast.5, bf16[48,128]{1,0:T(8,128)(2,1)} %bitcast.7, bf16[128,128]{1,0:T(8,128)(2,1)} %second_ref.1, bf16[32,128]{1,0:T(8,128)(2,1)} %third_ref.1, ...), custom_call_target="tpu_custom_call" | custom-call | tf_op jit(solution)/shard_map/pallas_call | solution.py:596
  28.9 1.3 %copy.12 = f32[3,8,64]{2,1,0:T(8,128)} copy(f32[3,8,64]{2,1,0:T(8,128)} %shard_map.100) | data formatting | bytes 12288

commit v2 on v1

--- a/solution.py
+++ b/solution.py
@@ -159,10 +159,20 @@
     return device + 1 - 2 * (device % 2)
 
 
+def staged(count, bands, scaling, *refs):
+    sources, held, load_sem = refs[:10], refs[-11:-1], refs[-1]
+    loads = [
+        pltpu.make_async_copy(source, target, load_sem.at[place])
+        for place, (source, target) in enumerate(zip(sources, held))
+    ]
+    fused(count, bands, scaling, loads, *held, *refs[10:-11])
+
+
 def fused(
     count,
     bands,
     scaling,
+    loads,
     feat_ref,
     rad_ref,
     order_ref,
@@ -223,24 +233,16 @@
 
     @pl.when(has_above)
     def _():
-        for peer in [me] + peers:
-            pl.semaphore_signal(
-                barrier,
-                inc=1,
-                device_id={"samp": peer, "band": here - 1},
-                device_id_type=MESH,
-            )
+        pl.semaphore_signal(barrier, inc=1, device_id={"band": here - 1}, device_id_type=MESH)
 
     @pl.when(has_below)
     def _():
-        for peer in [me] + peers:
-            pl.semaphore_signal(
-                barrier,
-                inc=1,
-                device_id={"samp": peer, "band": here + 1},
-                device_id_type=MESH,
-            )
-
+        pl.semaphore_signal(barrier, inc=1, device_id={"band": here + 1}, device_id_type=MESH)
+
+    for place in (2, 0, 3, 4, 5, 1, 6, 8, 7, 9):
+        loads[place].start()
+
+    loads[2].wait()
     source = slots_to_sources(order_ref[0], width)
     halves = []
     for start in range(0, width, lanes):
@@ -260,12 +262,16 @@
             axis=1,
         )
 
+    loads[0].wait()
     for chan in range(channels):
         for half, part_x in enumerate(reorder(feat_ref[chan, 0].astype(jnp.float32))):
             plane[half, chan * rows : (chan + 1) * rows, :] = part_x
+    loads[1].wait()
     for chan in range(3):
         light[chan] = jnp.concatenate(reorder(rad_ref[chan, 0]), axis=1)
 
+    for place in (3, 4, 5):
+        loads[place].wait()
     first_ref[...] = first_turned[...].T
 
     def embed_row(row):
@@ -278,49 +284,55 @@
         emb_bf[row] = x.astype(jnp.bfloat16)
         return x
 
-    beside = jnp.minimum(here, 1) + jnp.minimum(bands - 1 - here, 1)
-    sums = []
     for slot, peer in enumerate(peers):
         start = share_of(peer, count) * share
         for row in range(share):
             part[slot, row] = embed_row(start + row).astype(part.dtype)
-        if slot == 0:
-            pl.semaphore_wait(barrier, count - 1 + beside * count)
-        copy = pltpu.make_async_remote_copy(
-            src_ref=part.at[slot],
-            dst_ref=part_in.at[slot],
-            send_sem=rs_send.at[slot],
-            recv_sem=rs_recv.at[slot],
+    total = [embed_row(chunk * share + row) for row in range(share)]
+    for place in (6, 8, 7, 9):
+        loads[place].wait()
+    conv_one_ref[...] = conv_one_turned[...].T
+    kern_one_ref[...] = kern_one_turned[...].T
+    canvas[...] = jnp.zeros(canvas.shape, jnp.float32)
+
+    beside = jnp.minimum(here, 1) + jnp.minimum(bands - 1 - here, 1)
+    pl.semaphore_wait(barrier, count - 1 + beside)
+    sums = []
+    for row in range(share):
+        for slot, peer in enumerate(peers):
+            copy = pltpu.make_async_remote_copy(
+                src_ref=part.at[slot, row],
+                dst_ref=part_in.at[slot, row],
+                send_sem=rs_send.at[slot, row],
+                recv_sem=rs_recv.at[slot, row],
+                device_id={"samp": peer},
+                device_id_type=MESH,
+            )
+            copy.start()
+            sums.append(copy)
+
+    def gather(slot, row, peer, sender):
+        at = radius + share_of(sender, count) * share + row
+        return pltpu.make_async_remote_copy(
+            src_ref=pooled.at[at],
+            dst_ref=pooled.at[at],
+            send_sem=ag_send.at[slot, row],
+            recv_sem=ag_recv.at[sender, row],
             device_id={"samp": peer},
             device_id_type=MESH,
         )
-        copy.start()
-        sums.append(copy)
-    total = [embed_row(chunk * share + row) for row in range(share)]
-    conv_one_ref[...] = conv_one_turned[...].T
-    kern_one_ref[...] = kern_one_turned[...].T
-    canvas[...] = jnp.zeros(canvas.shape, jnp.float32)
-    for slot, copy in enumerate(sums):
-        copy.wait_recv()
-        for row in range(share):
-            total[row] = total[row] + part_in[slot, row].astype(jnp.float32)
+
+    gathers = []
     for row in range(share):
-        pooled[radius + chunk * share + row] = (total[row] * scaling).astype(jnp.bfloat16)
-
-    def gather(slot, peer, sender):
-        rows_of = pl.ds(radius + share_of(sender, count) * share, share)
-        return pltpu.make_async_remote_copy(
-            src_ref=pooled.at[rows_of],
-            dst_ref=pooled.at[rows_of],
-            send_sem=ag_send.at[slot],
-            recv_sem=ag_recv.at[sender],
-            device_id={"samp": peer},
-            device_id_type=MESH,
-        )
-
-    gathers = [gather(slot, peer, me) for slot, peer in enumerate(peers)]
-    for copy in gathers:
-        copy.start()
+        summed = total[row]
+        for slot in range(count - 1):
+            sums[row * (count - 1) + slot].wait_recv()
+            summed = summed + part_in[slot, row].astype(jnp.float32)
+        pooled[radius + chunk * share + row] = (summed * scaling).astype(jnp.bfloat16)
+        for slot, peer in enumerate(peers):
+            copy = gather(slot, row, peer, me)
+            copy.start()
+            gathers.append(copy)
 
     def halo(down):
         start = rows if down else radius
@@ -381,7 +393,8 @@
 
         @pl.when(me != owner)
         def _():
-            gather(0, peers[0], owner).wait_recv()
+            for row in range(share):
+                gather(0, row, peers[0], owner).wait_recv()
 
         if place == edges - 1:
 
@@ -591,12 +604,24 @@
     taps_pad = -(-KSIZE * KSIZE // 8) * 8
     scaling = 1.0 / math.sqrt(samples_dev * count)
     vmem = pl.BlockSpec(memory_space=pltpu.VMEM)
+    operands = (
+        features,
+        radiance,
+        jnp.swapaxes(sample_order, 2, 3),
+        embed_first.T,
+        embed_second,
+        embed_third,
+        conv_first.T,
+        conv_second,
+        kernel_first.T,
+        kernel_second,
+    )
     sem = pltpu.SemaphoreType.DMA
     rim_rows = -(-groups * radius // 8) * 8
     return pl.pallas_call(
-        functools.partial(fused, count, bands, scaling),
+        functools.partial(staged, count, bands, scaling),
         out_shape=jax.ShapeDtypeStruct((3, rows, cols), jnp.float32),
-        in_specs=[vmem] * 10,
+        in_specs=[pl.BlockSpec(memory_space=pl.ANY)] * len(operands),
         out_specs=vmem,
         scratch_shapes=[
             pltpu.VMEM(embed_first.shape, jnp.bfloat16),
@@ -615,30 +640,21 @@
             pltpu.VMEM((count - 1, groups * rows, LANES), jnp.float32),
             pltpu.VMEM((2, count, rim_rows, LANES), jnp.float32),
             pltpu.VMEM((2, count, rim_rows, LANES), jnp.float32),
-            sem((count - 1,)),
-            sem((count - 1,)),
-            sem((count - 1,)),
-            sem((count,)),
+            sem((count - 1, rows // count)),
+            sem((count - 1, rows // count)),
+            sem((count - 1, rows // count)),
+            sem((count, rows // count)),
             sem((2,)),
             sem((2,)),
             sem((count - 1,)),
             sem((count - 1,)),
             sem((2, count)),
             sem((2, count)),
+            *[pltpu.VMEM(value.shape, value.dtype) for value in operands],
+            sem((len(operands),)),
         ],
         compiler_params=pltpu.CompilerParams(collective_id=0, has_side_effects=True),
-    )(
-        features,
-        radiance,
-        jnp.swapaxes(sample_order, 2, 3),
-        embed_first.T,
-        embed_second,
-        embed_third,
-        conv_first.T,
-        conv_second,
-        kernel_first.T,
-        kernel_second,
-    )
+    )(*operands)
 
 
 def either(*operands):

time: 30.4 us -> 30 us (0.987)
  the two profiles are of different devices: /device:TPU:0 before, /device:TPU:1 now
where the time goes in v2:
time: 30 us; the launch traced here: 29.8 us
  Pallas kernels  28.5 us (95%)
  local copies, waits for them, and re-layouts  1.31 us (4%)
    pallas_call x1, Pallas kernels, fused_shards(): pl.pallas_call(functools.partial(staged, count, bands, scaling), out_shap...  28.5 us
    unnamed x1, local copies, waits for them, and re-layouts  1.31 us

profile of v2, /device:TPU:1, one launch (start us, length us, event | category | flops | bytes accessed | tf_op | source)
XLA Modules:
  0.0 29.8 jit_solution(11817403470036103774)
XLA Ops:
  0.0 28.5 %shard_map.100 = f32[3,8,64]{2,1,0:T(8,128)} custom-call(bf16[48,1,8,256]{3,2,1,0:T(8,128)(2,1)} %refs_0_.1, f32[3,1,8,256]{3,2,1,0:T(8,128)} %refs_1_.1, s32[1,8,8,32]{3,2,1,0:T(8,128)} %bitcast.5, bf16[48,128]{1,0:T(8,128)(2,1)} %bitcast.7, bf16[128,128]{1,0:T(8,128)(2,1)} %refs_4_.1, bf16[32,128]{1,0:T(8,128)(2,1)} %refs_5_.1, bf16[800,128]{1,0:T(8,128)(2,1)} %bitcast.4, ...), custom_call_target="tpu_custom_call" | custom-call | tf_op jit(solution)/shard_map/pallas_call | solution.py:621
  28.5 1.3 %copy.12 = f32[3,8,64]{2,1,0:T(8,128)} copy(f32[3,8,64]{2,1,0:T(8,128)} %shard_map.100) | data formatting | bytes 12288

commit v3 on v2

--- a/solution.py
+++ b/solution.py
@@ -266,9 +266,6 @@
     for chan in range(channels):
         for half, part_x in enumerate(reorder(feat_ref[chan, 0].astype(jnp.float32))):
             plane[half, chan * rows : (chan + 1) * rows, :] = part_x
-    loads[1].wait()
-    for chan in range(3):
-        light[chan] = jnp.concatenate(reorder(rad_ref[chan, 0]), axis=1)
 
     for place in (3, 4, 5):
         loads[place].wait()
@@ -284,22 +281,13 @@
         emb_bf[row] = x.astype(jnp.bfloat16)
         return x
 
-    for slot, peer in enumerate(peers):
-        start = share_of(peer, count) * share
-        for row in range(share):
-            part[slot, row] = embed_row(start + row).astype(part.dtype)
-    total = [embed_row(chunk * share + row) for row in range(share)]
-    for place in (6, 8, 7, 9):
-        loads[place].wait()
-    conv_one_ref[...] = conv_one_turned[...].T
-    kern_one_ref[...] = kern_one_turned[...].T
-    canvas[...] = jnp.zeros(canvas.shape, jnp.float32)
-
     beside = jnp.minimum(here, 1) + jnp.minimum(bands - 1 - here, 1)
-    pl.semaphore_wait(barrier, count - 1 + beside)
     sums = []
     for row in range(share):
         for slot, peer in enumerate(peers):
+            part[slot, row] = embed_row(share_of(peer, count) * share + row).astype(part.dtype)
+            if not sums:
+                pl.semaphore_wait(barrier, count - 1 + beside)
             copy = pltpu.make_async_remote_copy(
                 src_ref=part.at[slot, row],
                 dst_ref=part_in.at[slot, row],
@@ -310,6 +298,15 @@
             )
             copy.start()
             sums.append(copy)
+    total = [embed_row(chunk * share + row) for row in range(share)]
+    loads[1].wait()
+    for chan in range(3):
+        light[chan] = jnp.concatenate(reorder(rad_ref[chan, 0]), axis=1)
+    for place in (6, 8, 7, 9):
+        loads[place].wait()
+    conv_one_ref[...] = conv_one_turned[...].T
+    kern_one_ref[...] = kern_one_turned[...].T
+    canvas[...] = jnp.zeros(canvas.shape, jnp.float32)
 
     def gather(slot, row, peer, sender):
         at = radius + share_of(sender, count) * share + row

time: 30 us -> 28.6 us (0.953)
  Pallas kernels: 28.5 us -> 26.9 us
    pallas_call x1, Pallas kernels: 28.5 us -> 26.9 us  [fused_shards(): pl.pallas_call(functools.partial(staged, count, bands, scaling), out_shap...]
where the time goes in v3:
time: 28.6 us; the launch traced here: 28.2 us
  Pallas kernels  26.9 us (94%)
  local copies, waits for them, and re-layouts  1.31 us (5%)
    pallas_call x1, Pallas kernels, fused_shards(): pl.pallas_call(functools.partial(staged, count, bands, scaling), out_shap...  26.9 us
    unnamed x1, local copies, waits for them, and re-layouts  1.31 us

profile of v3, /device:TPU:1, one launch (start us, length us, event | category | flops | bytes accessed | tf_op | source)
XLA Modules:
  0.0 28.2 jit_solution(15157927909695095471)
XLA Ops:
  0.0 26.9 %shard_map.100 = f32[3,8,64]{2,1,0:T(8,128)} custom-call(bf16[48,1,8,256]{3,2,1,0:T(8,128)(2,1)} %refs_0_.1, f32[3,1,8,256]{3,2,1,0:T(8,128)} %refs_1_.1, s32[1,8,8,32]{3,2,1,0:T(8,128)} %bitcast.5, bf16[48,128]{1,0:T(8,128)(2,1)} %bitcast.7, bf16[128,128]{1,0:T(8,128)(2,1)} %refs_4_.1, bf16[32,128]{1,0:T(8,128)(2,1)} %refs_5_.1, bf16[800,128]{1,0:T(8,128)(2,1)} %bitcast.4, ...), custom_call_target="tpu_custom_call" | custom-call | tf_op jit(solution)/shard_map/pallas_call | solution.py:618
  26.9 1.3 %copy.12 = f32[3,8,64]{2,1,0:T(8,128)} copy(f32[3,8,64]{2,1,0:T(8,128)} %shard_map.100) | data formatting | bytes 12288
